TPU v7x, 32 devices: a whole 2x2x4 slice. The times are simulated.
32 devices in a mesh: section: 4 (over y, x), ctx: 8 (over z, core).
Axes of the slice: x: 2, y: 2, z: 4, core: 2. Of those that a mesh axis runs over, the one named last changes fastest.
Arguments:
- resid: bfloat16 [4, 1024, 6144], P('section', 'ctx'), may hold values from -6 to 6
- queries: bfloat16 [4, 1024, 6144], P('section', 'ctx'), may hold values from -6 to 6
- keys: bfloat16 [4, 1024, 6144], P('section', 'ctx'), may hold values from -6 to 6
- values: bfloat16 [4, 1024, 6144], P('section', 'ctx'), may hold values from -6 to 6
- log_decay: float32 [4, 1024, 48], P('section', 'ctx'), may hold values from -3 to 0
- attn_gain: float32 [4, 6144], P('section'), may hold values from 0.25 to 1.75
- moe_gain: float32 [4, 6144], P('section'), may hold values from 0.25 to 1.75
- experts: int32 [4, 1024, 2], P('section', 'ctx'), may hold values from 0 to 31, all different within a row; in each aligned block of 128 rows (0 to 127, 128 to 255, ..., all dimensions but the last counted through in order) at most 16 rows name the same one
- combine_weight: float32 [4, 1024, 2], P('section', 'ctx'), may hold values from 0.2 to 1
- w_up: bfloat16 [4, 6144, 5120], P('section', None, 'ctx'), may hold values from -0.078125 to 0.078125
- w_down: bfloat16 [4, 5120, 6144], P('section', 'ctx'), may hold values from -0.078125 to 0.078125
Outputs:
- received: bfloat16 [4, 1024, 6144], P('section', 'ctx')
Inputs may be any that keep to these rules, and one draw needn't show every extreme that they name: In the rows of one device each expert is named at most 16 times, and the two experts of a token differ.
All inputs are finite; a program needn't handle non-finite values.
Results may differ from a plain program's by a relative error of at most 0.002.
Values may be sent and summed in bfloat16 or wider, within the bound.
No kernel may reach another device: no remote copies, remote signals or barrier semaphores. Data moves between devices by JAX's collectives and lax.ppermute only.
A program may use at most 256 MiB of HBM per device.

v0:
```python
import jax
import jax.numpy as jnp
from jax import lax
from jax.sharding import PartitionSpec as P

D = 6144
LINEAR_HEADS = 48
HEAD = 128
EXPERTS = 32
SHARDS = 8
CAP_SRC = 16
HIGH = lax.Precision.HIGHEST


def prefix_2(part, axis, combine, identity):
    place = lax.axis_index(axis)
    gathered = jax.tree.map(lambda a: lax.all_gather(a, axis), part)
    state = jax.tree.map(lambda a, e: jnp.zeros_like(a) + jnp.asarray(e, a.dtype), part, identity)

    def one(step, state):
        return combine(
            state, jax.tree.map(lambda a: lax.dynamic_index_in_dim(a, step, 0, False), gathered)
        )

    return lax.fori_loop(0, place, one, state)


def passed_along(value, axis, steps):
    count = lax.axis_size(axis)
    pairs = [(source, (source + steps) % count) for source in range(count)]
    return lax.ppermute(value, axis, pairs)


def rms_scale(values_in, gain):
    return (
        values_in
        * lax.rsqrt(jnp.mean(values_in * values_in, axis=-1, keepdims=True) + 1e-06)
        * gain
    )


def slots_of(chosen):
    onehot = (chosen[:, None] == jnp.arange(EXPERTS)[None, :]).astype(jnp.int32)
    before = jnp.cumsum(onehot, axis=0) - onehot
    return jnp.sum(before * onehot, axis=1)


def join_states(earlier, later):
    return (earlier[0] * later[0], later[0][:, None, None] * earlier[1] + later[1])


def local(
    resid,
    queries,
    keys,
    values,
    log_decay,
    attn_gain,
    moe_gain,
    experts,
    combine_weight,
    w_up,
    w_down,
):
    length = queries.shape[1]
    query = queries[0].astype(jnp.float32).reshape(length, LINEAR_HEADS, HEAD)
    keyrows = keys[0].astype(jnp.float32).reshape(length, LINEAR_HEADS, HEAD)
    valrows = values[0].astype(jnp.float32).reshape(length, LINEAR_HEADS, HEAD)
    log_rate = log_decay[0]
    cumul = jnp.cumsum(log_rate, axis=0)
    scores = jnp.einsum("thd,shd->hts", query, keyrows, precision=HIGH)
    spread = cumul.T[:, :, None] - cumul.T[:, None, :]
    lower = jnp.arange(length)[:, None] >= jnp.arange(length)[None, :]
    weights = jnp.exp(jnp.where(lower[None], spread, -1e30))
    intra = jnp.einsum("hts,shd->thd", scores * weights, valrows, precision=HIGH)
    tail_decay = jnp.exp(cumul[-1][None, :] - cumul)
    state = jnp.einsum("thd,the->hde", keyrows * tail_decay[:, :, None], valrows, precision=HIGH)
    identity = (
        jnp.ones((LINEAR_HEADS,), jnp.float32),
        jnp.zeros((LINEAR_HEADS, HEAD, HEAD), jnp.float32),
    )
    prefix = prefix_2((jnp.exp(cumul[-1]), state), "ctx", join_states, identity)
    inter = jnp.exp(cumul)[:, :, None] * jnp.einsum(
        "thd,hde->the", query, prefix[1], precision=HIGH
    )
    attn_raw = (intra + inter).reshape(length, D)
    hres = resid[0].astype(jnp.float32) + rms_scale(attn_raw, attn_gain[0])
    normed = rms_scale(hres, moe_gain[0]).astype(jnp.bfloat16)
    ctx_count = lax.axis_size("ctx")
    flying = ctx_count // SHARDS
    my_expert = lax.axis_index("ctx") // SHARDS
    chosen = experts[0].reshape(-1)
    slot = slots_of(chosen)
    target = chosen * CAP_SRC + slot
    in_window = chosen < flying
    select = (
        (target[None, :] == jnp.arange(flying * CAP_SRC)[:, None]) & in_window[None, :]
    ).astype(jnp.bfloat16)
    doubled = jnp.repeat(normed, 2, axis=0)
    outbox = jnp.dot(select, doubled, preferred_element_type=jnp.float32).astype(jnp.bfloat16)
    outbox = outbox.reshape(flying, CAP_SRC, D)
    up_local = w_up[0]
    down_local = w_down[0]
    mine = lax.dynamic_index_in_dim(
        lax.all_gather(outbox[None], "ctx", axis=0, tiled=True), my_expert, 1, False
    )
    count = mine.shape[0]
    hidden = jax.nn.gelu(
        jnp.dot(mine.reshape(count * CAP_SRC, D), up_local, preferred_element_type=jnp.float32),
        approximate=True,
    ).astype(jnp.bfloat16)
    partial_value = (
        jnp.dot(hidden, down_local, preferred_element_type=jnp.float32)
        .astype(jnp.bfloat16)
        .reshape(count, CAP_SRC, D)
    )
    returned = lax.all_to_all(partial_value, "ctx", split_axis=0, concat_axis=0, tiled=True)
    summed = returned.reshape(flying, SHARDS, CAP_SRC, D).astype(jnp.float32).sum(axis=1)
    summed = summed.reshape(flying * CAP_SRC, D)
    picked = jnp.take(summed, jnp.clip(target, 0, flying * CAP_SRC - 1), axis=0)
    picked = jnp.where(in_window[:, None], picked, 0.0) * combine_weight[0].reshape(-1)[:, None]
    mixed = picked.reshape(length, 2, D).sum(axis=1)
    layer_out = (hres + mixed).astype(jnp.bfloat16)
    return passed_along(layer_out[None], "section", 1)


def solution(mesh):
    return jax.shard_map(
        local,
        mesh=mesh,
        in_specs=(
            P("section", "ctx", None),
            P("section", "ctx", None),
            P("section", "ctx", None),
            P("section", "ctx", None),
            P("section", "ctx", None),
            P("section", None),
            P("section", None),
            P("section", "ctx", None),
            P("section", "ctx", None),
            P("section", None, "ctx"),
            P("section", "ctx", None),
        ),
        out_specs=P("section", "ctx", None),
        check_vma=False,
    )
```

profile of v0, /device:TPU:0, one launch (start us, length us, event | category | flops | bytes accessed | tf_op | source)
XLA Modules:
  0.0 450.4 jit_solution(3672909860523334791)
XLA Ops:
  6.5 0.9 copy.47
  7.8 1.9 copy.66
  10.1 1.2 copy-done.2
  11.3 3.6 fusion.11
  15.1 0.6 copy-done.11
  16.1 1.8 copy.68
  18.0 0.6 reduce-window.6
  18.8 13.5 %all-gather.2 = f32[8,1,48]{2,1,0:T(1,128)S(1)} all-gather(f32[1,1,48]{2,1,0:T(1,128)S(1)} %get-tuple-element.63), channel_id=1, replica_groups=mesh['section'=4,'ctx'=8] {'ctx'}, dimensions={0}, use_global_device_ids=true | all-gather | bytes 1728 | tf_op jit(solution)/shard_map/all_gather | solution.py:17
  32.4 0.6 fusion.27
  33.0 0.9 copy-done.3
  34.0 5.5 %fusion.14 = f32[48,128,128]{1,2,0:T(8,128)} fusion(f32[48,128,128]{2,1,0:T(8,128)S(1)} %fusion.27, f32[48,128]{1,0:T(8,128)S(1)} %copy.48, pred[128,128]{1,0:T(8,128)(4,1)S(1)} %iota_compare_fusion, bf16[128,48,128]{2,1,0:T(8,128)(2,1)S(1)} %bitcast.101), kind=kOutput, calls=%fused_computation.24 | convolution fusion | flops 1210318848 | bytes 7905280 | tf_op jit(solution)/shard_map/hts,shd->thd/dot_general | solution.py:75
  39.4 198.3 %all-gather.6.cloned.1.call-done = f32[384,128,128]{2,1,0:T(8,128)} async-done(((f32[48,128,128]{2,1,0:T(8,128)}), f32[384,128,128]{2,1,0:T(8,128)}) %all-gather.6.cloned.1.call-update) | async-done | bytes 25165840 | tf_op jit(solution)/shard_map/all_gather | solution.py:17
  238.3 6.8 %multiply_reduce_fusion.2 = (f32[128]{0:T(128)S(1)}, f32[128,48,128]{0,2,1:T(8,128)}) fusion(f32[48,128,128]{2,1,0:T(8,128)S(1)} %get-tuple-element.49, bf16[128,48,128]{2,1,0:T(8,128)(2,1)} %bitcast.97, f32[128,48]{0,1:T(8,128)S(1)} %copy.51, f32[48,128,128]{1,2,0:T(8,128)} %fusion.14), kind=kOutput, calls=%fused_computation.20 | convolution fusion | flops 1211105152 | bytes 11035136 | tf_op jit(solution)/shard_map/thd,hde->the/dot_general | solution.py:83
  245.1 2.4 copy.63
  247.5 2.3 multiply_reduce_fusion.1
  249.8 1.9 multiply_convert_fusion
  251.7 5.0 %broadcast_in_dim.63 = bf16[128,2,6144]{2,1,0:T(2,128)(2,1)} broadcast(bf16[128,6144]{1,0:T(8,128)(2,1)} %multiply_convert_fusion), dimensions={0,2} | broadcast | bytes 4718592 | tf_op jit(solution)/shard_map/broadcast_in_dim | solution.py:99
  256.7 6.2 %reshape.246 = bf16[256,6144]{1,0:T(8,128)(2,1)S(1)} reshape(bf16[128,2,6144]{2,1,0:T(2,128)(2,1)} %broadcast_in_dim.63) | data formatting | bytes 6291456 | tf_op jit(solution)/shard_map/reshape | solution.py:99
  262.9 1.2 convolution_convert_fusion
  264.1 40.8 %all-gather.8.cloned.1.call-done = bf16[128,6144]{1,0:T(8,128)(2,1)} async-done(((bf16[16,6144]{1,0:T(8,128)(2,1)}), bf16[128,6144]{1,0:T(8,128)(2,1)}) %all-gather.8.cloned.1.call-update) | async-done | bytes 1572880 | tf_op jit(solution)/shard_map/all_gather | solution.py:105
  304.9 9.8 %fusion.4 = bf16[128,6144]{1,0:T(8,128)(2,1)} fusion(bf16[1,640,6144]{2,1,0:T(8,128)(2,1)} %param.23, bf16[128,6144]{1,0:T(8,128)(2,1)} %all-gather.8.cloned.1.call-done, bf16[1,6144,640]{2,1,0:T(8,128)(2,1)} %param.22), kind=kOutput, calls=%fused_computation.7 | convolution fusion | flops 2014789632 | bytes 18874368 | tf_op jit(solution)/shard_map/dot_general | solution.py:113
  314.7 4.8 %all-to-all-start = ((bf16[8,16,6144]{2,1,0:T(8,128)(2,1)}), bf16[8,16,6144]{2,1,0:T(8,128)(2,1)}, u32[]{:S(2)}, u32[]{:S(2)}) async-start(bf16[8,16,6144]{2,1,0:T(8,128)(2,1)} %bitcast.103), calls=%async_computation | async-start | bytes 3145728 | tf_op jit(solution)/shard_map/all_to_all | solution.py:117
  320.1 2.4 copy.57
  322.5 34.6 %all-to-all-done = bf16[8,16,6144]{2,1,0:T(8,128)(2,1)} async-done(((bf16[8,16,6144]{2,1,0:T(8,128)(2,1)}), bf16[8,16,6144]{2,1,0:T(8,128)(2,1)}, u32[]{:S(2)}, u32[]{:S(2)}) %all-to-all-start) | async-done | bytes 1572896 | tf_op jit(solution)/shard_map/all_to_all | solution.py:117
  357.0 1.7 convert_reduce_fusion
  358.7 5.1 %gather_fusion = f32[256,6144]{1,0:T(8,128)} fusion(f32[16,6144]{1,0:T(8,128)S(1)} %convert_reduce_fusion, s32[1024]{0:T(1024)S(1)} %pad_clamp_fusion), kind=kCustom, calls=%fused_computation | custom fusion | bytes 12583936 | tf_op jit(solution)/shard_map/jit(_take)/gather | solution.py:120
  363.8 8.1 %gather.7 = f32[128,2,6144]{2,1,0:T(2,128)} reshape(f32[256,6144]{1,0:T(8,128)} %gather_fusion) | data formatting | bytes 12582912 | tf_op jit(solution)/shard_map/jit(_take)/gather | solution.py:120
  372.0 32.9 %multiply_reduce_fusion = f32[128,6144]{1,0:T(8,128)S(1)} fusion(f32[128,2,6144]{2,1,0:T(2,128)} %gather.7, pred[128,2]{1,0:T(8,128)(4,1)S(1)} %compare_and_fusion, pred[128,2]{1,0:T(8,128)(4,1)S(1)} %copy.58, f32[128,2]{1,0:T(8,128)S(1)} %copy.64), kind=kLoop, calls=%fused_computation.9 | loop fusion | flops 5505024 | bytes 9438720 | tf_op jit(solution)/shard_map/reduce_sum | solution.py:122
  404.9 0.7 fusion.8
  405.6 1.5 collective-permute-start
  407.1 35.3 %collective-permute-done = bf16[1,128,6144]{2,1,0:T(8,128)(2,1)S(1)} collective-permute-done((bf16[1,128,6144]{2,1,0:T(8,128)(2,1)S(1)}, bf16[1,128,6144]{2,1,0:T(8,128)(2,1)S(1)}, u32[]{:S(2)}, u32[]{:S(2)}) %collective-permute-start) | collective-permute-done | bytes 1572896 | tf_op jit(solution)/shard_map/ppermute | solution.py:31
  442.4 1.1 copy.88
  (56 shorter events, 2.8 us)
Async XLA Ops:
  6.5 3.2 copy-start.7
  6.5 231.2 %all-gather.6.cloned.1.call-start = ((), (), s32[]{:S(2)}) async-start(), calls=%async_computation.1 | async-start | bytes 28311552 | tf_op jit(solution)/shard_map/all_gather | solution.py:17
  10.1 1.2 copy-start.2
  15.0 0.7 copy-start.11
  15.0 289.9 %all-gather.8.cloned.1.call-start = ((), (), s32[]{:S(2)}) async-start(), calls=%async_computation.2 | async-start | bytes 1769472 | tf_op jit(solution)/shard_map/all_gather | solution.py:105
  17.9 15.1 %copy-start.1 = (bf16[16,8,48,128]{3,2,1,0:T(8,128)(2,1)}, bf16[16,8,48,128]{3,2,1,0:T(8,128)(2,1)S(1)}, u32[]{:S(2)}) copy-start(bf16[16,8,48,128]{3,2,1,0:T(8,128)(2,1)S(1)} %copy.68) | copy-start | bytes 4718596
  32.4 1.5 copy-start.3
  245.1 2.4 copy-start.8
  247.5 2.4 copy-start.4
  247.5 2.3 copy-start.9
  314.7 5.1 %copy-start.10 = (f32[1,128,2]{1,2,0:T(2,128)S(1)}, f32[1,128,2]{1,2,0:T(2,128)}, u32[]{:S(2)}) copy-start(f32[1,128,2]{1,2,0:T(2,128)} %param.21) | copy-start | bytes 3076
  314.7 5.4 %copy-start = (f32[128,48,128]{0,2,1:T(8,128)S(1)}, f32[128,48,128]{0,2,1:T(8,128)}, u32[]{:S(2)}) copy-start(f32[128,48,128]{0,2,1:T(8,128)} %get-tuple-element.65) | copy-start | bytes 9437188
  314.7 42.4 %all-to-all-start = ((bf16[8,16,6144]{2,1,0:T(8,128)(2,1)}), bf16[8,16,6144]{2,1,0:T(8,128)(2,1)}, u32[]{:S(2)}, u32[]{:S(2)}) async-start(bf16[8,16,6144]{2,1,0:T(8,128)(2,1)} %bitcast.103), calls=%async_computation | async-start | bytes 3145728 | tf_op jit(solution)/shard_map/all_to_all | solution.py:117
  372.0 32.9 %copy-start.5 = (bf16[1,128,6144]{2,1,0:T(8,128)(2,1)S(1)}, bf16[1,128,6144]{2,1,0:T(8,128)(2,1)}, u32[]{:S(2)}) copy-start(bf16[1,128,6144]{2,1,0:T(8,128)(2,1)} %param.13) | copy-start | bytes 4718596
  372.0 32.9 %copy-start.6 = (f32[1,128,6144]{2,1,0:T(8,128)S(1)}, f32[1,128,6144]{2,1,0:T(8,128)}, u32[]{:S(2)}) copy-start(f32[1,128,6144]{2,1,0:T(8,128)} %copy.57) | copy-start | bytes 9437188
  405.6 36.8 %collective-permute-start = (bf16[1,128,6144]{2,1,0:T(8,128)(2,1)S(1)}, bf16[1,128,6144]{2,1,0:T(8,128)(2,1)S(1)}, u32[]{:S(2)}, u32[]{:S(2)}) collective-permute-start(bf16[1,128,6144]{2,1,0:T(8,128)(2,1)S(1)} %fusion.8), channel_id=1, source_target_pairs={{0,8},{8,16},{16,24},{24,0},{1,9},{9,17},{17,25},{25,1},{2,10},{10... | collective-permute-start | bytes 4718600 | tf_op jit(solution)/shard_map/ppermute | solution.py:31
Sparse Core Ops, SparseCore 0:
  15.1 222.5 all-gather.5
  264.2 40.6 all-gather.7
where the time goes:
time: 451 us; the launch traced here: 450 us
  waiting for transfers between devices  309 us (69%)
  other arithmetic  40.5 us (9%)
  local copies, waits for them, and re-layouts  39.8 us (9%)
  matrix products  27.4 us (6%)
  between operations  13.7 us (3%)
  blocking collectives  13.5 us (3%)
  starting transfers between devices  6.34 us (1%)
    all_gather x1, waiting for transfers between devices, prefix_2(): gathered = jax.tree.map(lambda a: lax.all_gather(a, axis), part)  198 us
    all_gather x1, waiting for transfers between devices, local(): lax.all_gather(outbox[None], 'ctx', axis=0, tiled=True)  40.8 us
    ppermute x1, waiting for transfers between devices, passed_along(): return lax.ppermute(value, axis, pairs)  35.3 us
    all_to_all x1, waiting for transfers between devices, local(): lax.all_to_all(partial_value, 'ctx', split_axis=0, concat_axis=0, tiled=T...  34.6 us
    reduce_sum x1, other arithmetic, local(): mixed = picked.reshape(length, 2, D).sum(axis=1)  32.9 us
    all_gather x1, blocking collectives, prefix_2(): gathered = jax.tree.map(lambda a: lax.all_gather(a, axis), part)  13.5 us
    gather x2, local copies, waits for them, and re-layouts, local(): picked = jnp.take(summed, jnp.clip(target, 0, flying * CAP_SRC - 1), axis=0)  13.3 us
    dot_general x1, matrix products, local(): jnp.dot(hidden, down_local, preferred_element_type=jnp.float32)  9.77 us
  transfers between devices with their start and end apart: 4, of which 4 were waited for; matrix products, arithmetic and copies ran while one was open for 3% of the time, Pallas kernels for 0%

commit v1 on v0

--- a/solution.py
+++ b/solution.py
@@ -10,6 +10,24 @@
 SHARDS = 8
 CAP_SRC = 16
 HIGH = lax.Precision.HIGHEST
+
+
+def panels_turn(base_x, where_dim):
+    b_now = list(base_x.shape[1:])
+    b_now[where_dim] *= base_x.shape[0]
+    return jnp.moveaxis(base_x, 0, where_dim).reshape(b_now)
+
+
+def bars_shape(my_data, device_axis):
+    nodes = lax.axis_size(device_axis)
+    f_now = my_data[None]
+    for j in range(nodes.bit_length() - 1):
+        y = 1 << j
+        reply = lax.ppermute(f_now, axis_name=device_axis, perm=[(m, m ^ y) for m in range(nodes)])
+        upper = jnp.stack([f_now, reply], axis=0)
+        r1 = lax.axis_index(device_axis) >> j & 1
+        f_now = jnp.where(r1 == 0, upper, upper[::-1]).reshape(-1, *my_data.shape)
+    return f_now
 
 
 def prefix_2(part, axis, combine, identity):
@@ -101,9 +119,11 @@
     outbox = outbox.reshape(flying, CAP_SRC, D)
     up_local = w_up[0]
     down_local = w_down[0]
-    mine = lax.dynamic_index_in_dim(
-        lax.all_gather(outbox[None], "ctx", axis=0, tiled=True), my_expert, 1, False
-    )
+
+    def _use_figure(own_rows, vals, dimension_no):
+        return panels_turn(bars_shape(own_rows, vals), dimension_no)
+
+    mine = lax.dynamic_index_in_dim(_use_figure(outbox[None], "ctx", 0), my_expert, 1, False)
     count = mine.shape[0]
     hidden = jax.nn.gelu(
         jnp.dot(mine.reshape(count * CAP_SRC, D), up_local, preferred_element_type=jnp.float32),

time: 451 us -> 474 us (1.051)
  starting transfers between devices: 6.34 us -> 25.5 us
    ppermute x0 -> x3, waiting for transfers between devices: none -> 45.1 us  [bars_shape(): lax.ppermute(f_now, axis_name=device_axis, perm=[(m, m ^ y) for m in rang...]
    all_gather x1 -> x0, waiting for transfers between devices: 40.8 us -> none  [local(): lax.all_gather(outbox[None], 'ctx', axis=0, tiled=True)]
    ppermute x0 -> x3, starting transfers between devices: none -> 18.7 us  [bars_shape(): lax.ppermute(f_now, axis_name=device_axis, perm=[(m, m ^ y) for m in rang...]
  transfers between devices with their start and end apart: 4 -> 6, of which waited for: 4 -> 6; matrix products, arithmetic and copies ran while one was open for 3% -> 3% of each run, Pallas kernels for 0% -> 0%
where the time goes in v1:
time: 474 us
  waiting for transfers between devices  313 us (66%)
  other arithmetic  41.3 us (9%)
  local copies, waits for them, and re-layouts  39.9 us (8%)
  matrix products  26.3 us (6%)
  starting transfers between devices  25.5 us (5%)
  between operations  13.7 us (3%)
  blocking collectives  13.5 us (3%)
    all_gather x1, waiting for transfers between devices, prefix_2(): gathered = jax.tree.map(lambda a: lax.all_gather(a, axis), part)  198 us
    ppermute x3, waiting for transfers between devices, bars_shape(): lax.ppermute(f_now, axis_name=device_axis, perm=[(m, m ^ y) for m in rang...  45.1 us
    ppermute x1, waiting for transfers between devices, passed_along(): return lax.ppermute(value, axis, pairs)  35.1 us
    all_to_all x1, waiting for transfers between devices, local(): lax.all_to_all(partial_value, 'ctx', split_axis=0, concat_axis=0, tiled=T...  34.9 us
    reduce_sum x1, other arithmetic, local(): mixed = picked.reshape(length, 2, D).sum(axis=1)  32.9 us
    ppermute x3, starting transfers between devices, bars_shape(): lax.ppermute(f_now, axis_name=device_axis, perm=[(m, m ^ y) for m in rang...  18.7 us
    all_gather x1, blocking collectives, prefix_2(): gathered = jax.tree.map(lambda a: lax.all_gather(a, axis), part)  13.5 us
    gather x2, local copies, waits for them, and re-layouts, local(): picked = jnp.take(summed, jnp.clip(target, 0, flying * CAP_SRC - 1), axis=0)  13.3 us
  transfers between devices with their start and end apart: 6, of which 6 were waited for; matrix products, arithmetic and copies ran while one was open for 3% of the time, Pallas kernels for 0%

profile of v1, /device:TPU:0, one launch (start us, length us, event | category | flops | bytes accessed | tf_op | source)
XLA Modules:
  0.0 473.6 jit_solution(9470103437876923016)
XLA Ops:
  6.5 0.9 copy.47
  7.8 1.9 copy.66
  10.1 1.2 copy-done.2
  11.3 3.6 fusion.11
  16.1 1.8 copy.68
  18.8 13.5 %all-gather.1 = f32[8,1,48]{2,1,0:T(1,128)S(1)} all-gather(f32[1,1,48]{2,1,0:T(1,128)S(1)} %get-tuple-element.65), channel_id=1, replica_groups=mesh['section'=4,'ctx'=8] {'ctx'}, dimensions={0}, use_global_device_ids=true | all-gather | bytes 1728 | tf_op jit(solution)/shard_map/all_gather | solution.py:35
  33.0 0.9 copy-done.3
  34.0 5.5 %fusion.14 = f32[48,128,128]{1,2,0:T(8,128)} fusion(f32[48,128,128]{2,1,0:T(8,128)S(1)} %fusion.27, f32[48,128]{1,0:T(8,128)S(1)} %copy.48, pred[128,128]{1,0:T(8,128)(4,1)S(1)} %iota_compare_fusion, bf16[128,48,128]{2,1,0:T(8,128)(2,1)S(1)} %bitcast.113), kind=kOutput, calls=%fused_computation.24 | convolution fusion | flops 1210318848 | bytes 7905280 | tf_op jit(solution)/shard_map/hts,shd->thd/dot_general | solution.py:93
  39.4 198.3 %all-gather.4.cloned.1.call-done = f32[384,128,128]{2,1,0:T(8,128)} async-done(((f32[48,128,128]{2,1,0:T(8,128)}), f32[384,128,128]{2,1,0:T(8,128)}) %all-gather.4.cloned.1.call-update) | async-done | bytes 25165840 | tf_op jit(solution)/shard_map/all_gather | solution.py:35
  238.3 6.8 %multiply_reduce_fusion.2 = (f32[128]{0:T(128)S(1)}, f32[128,48,128]{0,2,1:T(8,128)}) fusion(f32[48,128,128]{2,1,0:T(8,128)S(1)} %get-tuple-element.49, bf16[128,48,128]{2,1,0:T(8,128)(2,1)} %bitcast.109, f32[128,48]{0,1:T(8,128)S(1)} %copy.51, f32[48,128,128]{1,2,0:T(8,128)} %fusion.14), kind=kOutput, calls=%fused_computation.20 | convolution fusion | flops 1211105152 | bytes 11035136 | tf_op jit(solution)/shard_map/thd,hde->the/dot_general | solution.py:101
  245.1 2.4 copy.63
  247.5 2.3 multiply_reduce_fusion.1
  249.8 1.9 multiply_convert_fusion
  251.7 5.0 %broadcast_in_dim.63 = bf16[128,2,6144]{2,1,0:T(2,128)(2,1)} broadcast(bf16[128,6144]{1,0:T(8,128)(2,1)} %multiply_convert_fusion), dimensions={0,2} | broadcast | bytes 4718592 | tf_op jit(solution)/shard_map/broadcast_in_dim | solution.py:117
  256.7 6.2 %reshape.253 = bf16[256,6144]{1,0:T(8,128)(2,1)S(1)} reshape(bf16[128,2,6144]{2,1,0:T(2,128)(2,1)} %broadcast_in_dim.63) | data formatting | bytes 6291456 | tf_op jit(solution)/shard_map/reshape | solution.py:117
  263.4 2.8 collective-permute-start
  266.2 1.1 collective-permute-done
  267.4 3.6 collective-permute-start.1
  270.9 9.7 %collective-permute-done.1 = bf16[2,1,1,16,6144]{4,3,0,2,1:T(8,128)(2,1)S(1)} collective-permute-done((bf16[2,1,1,16,6144]{4,3,0,2,1:T(8,128)(2,1)S(1)}, bf16[2,1,1,16,6144]{4,3,0,2,1:T(8,128)(2,1)S(1)}, u32[]{:S(2)}, u32[]{:S(2)}) %collective-permute-start.1) | collective-permute-done | bytes 393248 | tf_op jit(solution)/shard_map/ppermute | solution.py:26
  280.8 12.3 %collective-permute-start.2 = (bf16[4,1,1,16,6144]{4,3,0,2,1:T(8,128)(2,1)S(1)}, bf16[4,1,1,16,6144]{4,3,0,2,1:T(8,128)(2,1)S(1)}, u32[]{:S(2)}, u32[]{:S(2)}) collective-permute-start(bf16[4,1,1,16,6144]{4,3,0,2,1:T(8,128)(2,1)S(1)} %bitcast.117), channel_id=1, source_target_pairs={{0,4},{1,5},{2,6},{3,7},{4,0},{5,1},{6,2},{7,3},{8,12},{9,13},{10,... | collective-permute-start | bytes 2359304 | tf_op jit(solution)/shard_map/ppermute | solution.py:26
  293.1 34.4 %collective-permute-done.2 = bf16[4,1,1,16,6144]{4,3,0,2,1:T(8,128)(2,1)S(1)} collective-permute-done((bf16[4,1,1,16,6144]{4,3,0,2,1:T(8,128)(2,1)S(1)}, bf16[4,1,1,16,6144]{4,3,0,2,1:T(8,128)(2,1)S(1)}, u32[]{:S(2)}, u32[]{:S(2)}) %collective-permute-start.2) | collective-permute-done | bytes 786464 | tf_op jit(solution)/shard_map/ppermute | solution.py:26
  328.0 9.3 %fusion.4 = bf16[128,6144]{1,0:T(8,128)(2,1)} fusion(bf16[1,640,6144]{2,1,0:T(8,128)(2,1)} %param.23, bf16[128,6144]{1,0:T(8,128)(2,1)S(1)} %bitcast.116, bf16[1,6144,640]{2,1,0:T(8,128)(2,1)} %param.22), kind=kOutput, calls=%fused_computation.7 | convolution fusion | flops 2014789632 | bytes 18874368 | tf_op jit(solution)/shard_map/dot_general | solution.py:133
  337.3 5.1 %all-to-all-start = ((bf16[8,16,6144]{2,1,0:T(8,128)(2,1)}), bf16[8,16,6144]{2,1,0:T(8,128)(2,1)}, u32[]{:S(2)}, u32[]{:S(2)}) async-start(bf16[8,16,6144]{2,1,0:T(8,128)(2,1)} %bitcast.115), calls=%async_computation | async-start | bytes 3145728 | tf_op jit(solution)/shard_map/all_to_all | solution.py:137
  343.0 2.4 copy.57
  345.4 34.9 %all-to-all-done = bf16[8,16,6144]{2,1,0:T(8,128)(2,1)} async-done(((bf16[8,16,6144]{2,1,0:T(8,128)(2,1)}), bf16[8,16,6144]{2,1,0:T(8,128)(2,1)}, u32[]{:S(2)}, u32[]{:S(2)}) %all-to-all-start) | async-done | bytes 1572896 | tf_op jit(solution)/shard_map/all_to_all | solution.py:137
  380.3 1.7 convert_reduce_fusion
  381.9 5.1 %gather_fusion = f32[256,6144]{1,0:T(8,128)} fusion(f32[16,6144]{1,0:T(8,128)S(1)} %convert_reduce_fusion, s32[1024]{0:T(1024)S(1)} %pad_clamp_fusion), kind=kCustom, calls=%fused_computation | custom fusion | bytes 12583936 | tf_op jit(solution)/shard_map/jit(_take)/gather | solution.py:140
  387.1 8.1 %gather.7 = f32[128,2,6144]{2,1,0:T(2,128)} reshape(f32[256,6144]{1,0:T(8,128)} %gather_fusion) | data formatting | bytes 12582912 | tf_op jit(solution)/shard_map/jit(_take)/gather | solution.py:140
  395.2 32.9 %multiply_reduce_fusion = f32[128,6144]{1,0:T(8,128)S(1)} fusion(f32[128,2,6144]{2,1,0:T(2,128)} %gather.7, pred[128,2]{1,0:T(8,128)(4,1)S(1)} %compare_and_fusion, pred[128,2]{1,0:T(8,128)(4,1)S(1)} %copy.58, f32[128,2]{1,0:T(8,128)S(1)} %copy.64), kind=kLoop, calls=%fused_computation.9 | loop fusion | flops 5505024 | bytes 9438720 | tf_op jit(solution)/shard_map/reduce_sum | solution.py:142
  428.8 1.7 collective-permute-start.3
  430.6 35.1 %collective-permute-done.3 = bf16[1,128,6144]{2,1,0:T(8,128)(2,1)S(1)} collective-permute-done((bf16[1,128,6144]{2,1,0:T(8,128)(2,1)S(1)}, bf16[1,128,6144]{2,1,0:T(8,128)(2,1)S(1)}, u32[]{:S(2)}, u32[]{:S(2)}) %collective-permute-start.3) | collective-permute-done | bytes 1572896 | tf_op jit(solution)/shard_map/ppermute | solution.py:49
  465.6 1.1 copy.88
  (65 shorter events, 6.6 us)
Async XLA Ops:
  6.5 3.2 copy-start.7
  6.5 231.2 %all-gather.4.cloned.1.call-start = ((), (), s32[]{:S(2)}) async-start(), calls=%async_computation.1 | async-start | bytes 28311552 | tf_op jit(solution)/shard_map/all_gather | solution.py:35
  10.1 1.2 copy-start.2
  15.0 0.7 copy-start.11
  17.9 15.1 %copy-start.1 = (bf16[16,8,48,128]{3,2,1,0:T(8,128)(2,1)}, bf16[16,8,48,128]{3,2,1,0:T(8,128)(2,1)S(1)}, u32[]{:S(2)}) copy-start(bf16[16,8,48,128]{3,2,1,0:T(8,128)(2,1)S(1)} %copy.68) | copy-start | bytes 4718596
  32.4 1.5 copy-start.3
  245.1 2.4 copy-start.8
  247.5 2.4 copy-start.4
  247.5 2.3 copy-start.9
  263.4 3.9 collective-permute-start
  267.4 13.2 %collective-permute-start.1 = (bf16[2,1,1,16,6144]{4,3,0,2,1:T(8,128)(2,1)S(1)}, bf16[2,1,1,16,6144]{4,3,0,2,1:T(8,128)(2,1)S(1)}, u32[]{:S(2)}, u32[]{:S(2)}) collective-permute-start(bf16[2,1,1,16,6144]{4,3,0,2,1:T(8,128)(2,1)S(1)} %get-tuple-element.61), channel_id=1, source_target_pairs={{0,2},{1,3},{2,0},{3,1},{4,6},{5,7},{6,4},{7,5},{8,10},{9,11},{10,... | collective-permute-start | bytes 1179656 | tf_op jit(solution)/shard_map/ppermute | solution.py:26
  280.8 46.7 %collective-permute-start.2 = (bf16[4,1,1,16,6144]{4,3,0,2,1:T(8,128)(2,1)S(1)}, bf16[4,1,1,16,6144]{4,3,0,2,1:T(8,128)(2,1)S(1)}, u32[]{:S(2)}, u32[]{:S(2)}) collective-permute-start(bf16[4,1,1,16,6144]{4,3,0,2,1:T(8,128)(2,1)S(1)} %bitcast.117), channel_id=1, source_target_pairs={{0,4},{1,5},{2,6},{3,7},{4,0},{5,1},{6,2},{7,3},{8,12},{9,13},{10,... | collective-permute-start | bytes 2359304 | tf_op jit(solution)/shard_map/ppermute | solution.py:26
  337.3 5.4 %copy-start.10 = (f32[1,128,2]{1,2,0:T(2,128)S(1)}, f32[1,128,2]{1,2,0:T(2,128)}, u32[]{:S(2)}) copy-start(f32[1,128,2]{1,2,0:T(2,128)} %param.21) | copy-start | bytes 3076
  337.3 5.7 %copy-start = (f32[128,48,128]{0,2,1:T(8,128)S(1)}, f32[128,48,128]{0,2,1:T(8,128)}, u32[]{:S(2)}) copy-start(f32[128,48,128]{0,2,1:T(8,128)} %get-tuple-element.67) | copy-start | bytes 9437188
  337.3 43.0 %all-to-all-start = ((bf16[8,16,6144]{2,1,0:T(8,128)(2,1)}), bf16[8,16,6144]{2,1,0:T(8,128)(2,1)}, u32[]{:S(2)}, u32[]{:S(2)}) async-start(bf16[8,16,6144]{2,1,0:T(8,128)(2,1)} %bitcast.115), calls=%async_computation | async-start | bytes 3145728 | tf_op jit(solution)/shard_map/all_to_all | solution.py:137
  395.2 32.9 %copy-start.5 = (bf16[1,128,6144]{2,1,0:T(8,128)(2,1)S(1)}, bf16[1,128,6144]{2,1,0:T(8,128)(2,1)}, u32[]{:S(2)}) copy-start(bf16[1,128,6144]{2,1,0:T(8,128)(2,1)} %param.13) | copy-start | bytes 4718596
  395.2 32.9 %copy-start.6 = (f32[1,128,6144]{2,1,0:T(8,128)S(1)}, f32[1,128,6144]{2,1,0:T(8,128)}, u32[]{:S(2)}) copy-start(f32[1,128,6144]{2,1,0:T(8,128)} %copy.57) | copy-start | bytes 9437188
  428.8 36.8 %collective-permute-start.3 = (bf16[1,128,6144]{2,1,0:T(8,128)(2,1)S(1)}, bf16[1,128,6144]{2,1,0:T(8,128)(2,1)S(1)}, u32[]{:S(2)}, u32[]{:S(2)}) collective-permute-start(bf16[1,128,6144]{2,1,0:T(8,128)(2,1)S(1)} %fusion.8), channel_id=1, source_target_pairs={{0,8},{8,16},{16,24},{24,0},{1,9},{9,17},{17,25},{25,1},{2,10},{10... | collective-permute-start | bytes 4718600 | tf_op jit(solution)/shard_map/ppermute | solution.py:49
Sparse Core Ops, SparseCore 0:
  15.1 222.5 all-gather.3
